TPU v7x, 32 devices: a whole 2x2x4 slice. The times are simulated.
32 devices in a mesh: row: 4 (over z), col: 2 (over x), rep: 4 (over y, core).
Axes of the slice: x: 2, y: 2, z: 4, core: 2. Of those that a mesh axis runs over, the one named last changes fastest.
Arguments:
- features: bfloat16 [8192, 256], P(('col', 'rep'), 'row'), may hold values from -6 to 6
- weight: bfloat16 [256, 256], replicated, may hold values from -0.375 to 0.375
- cotangent: bfloat16 [8192, 256], P(('row', 'col', 'rep')), may hold values from -6 to 6
- block_values: bfloat16 [4, 8, 128, 128, 128], P('row', ('col', 'rep')), may hold values from -0.0625 to 0.0625
- block_coords: int32 [4, 8, 128, 2], P('row', ('col', 'rep')), may hold values from 0 to 15, as said below
- block_counts: int32 [4, 8], P('row', ('col', 'rep')), may hold values from 1 to 128, as said below
Outputs:
- activations: bfloat16 [8192, 256], P(('row', 'col', 'rep'))
- input_grad: bfloat16 [8192, 256], P(('col', 'rep'), 'row')
- weight_grad: float32 [256, 256], replicated
Inputs may be any that keep to these rules, and one draw needn't show every extreme that they name: `block_coords`: each slot's row block is below 16 and its column block below 8. `block_counts`: some tile uses all 128 slots.
All inputs are finite; a program needn't handle non-finite values.
Results may differ from a plain program's by a relative error of at most 0.014.
Values may be sent and summed in bfloat16 or wider, within the bound.
A program may use at most 128 MiB of HBM per device.

v0:
```python
import math

import jax
import jax.numpy as jnp
from jax import lax
from jax.sharding import PartitionSpec as P


def local(features, weight, cotangent, block_values, block_coords, block_counts):
    blocks = block_values[0, 0]
    coords = block_coords[0, 0]
    live_count = block_counts[0, 0]
    slots = blocks.shape[0]
    gathered = lax.all_gather(features, "row", axis=1, tiled=True)
    feat_width = gathered.shape[1]
    col_blocks = gathered.shape[0] // 128
    row_blocks = cotangent.shape[0] * lax.axis_size(("col", "rep")) // 128
    feat_blocks = gathered.reshape(col_blocks, 128, feat_width)
    is_live = (jnp.arange(slots, dtype=jnp.int32) < live_count).astype(jnp.float32)
    per_turn = math.gcd(slots, 64)
    rounds = slots // per_turn
    pieces = (
        blocks.reshape(rounds, per_turn, 128, 128),
        coords[:, 0].reshape(rounds, per_turn),
        coords[:, 1].reshape(rounds, per_turn),
        is_live.reshape(rounds, per_turn),
    )

    def forward_step(total, piece):
        blocks_g, rows_g, cols_g, live_g = piece
        chosen = feat_blocks[cols_g]
        product = jnp.einsum("bij,bjf->bif", blocks_g, chosen, preferred_element_type=jnp.float32)
        return (total.at[rows_g].add(product * live_g[:, None, None]), None)

    partial_value, _ = lax.scan(
        forward_step, jnp.zeros((row_blocks, 128, feat_width), jnp.float32), pieces
    )
    partial_value = partial_value.reshape(row_blocks * 128, feat_width)
    summed = lax.psum_scatter(partial_value, ("col", "rep"), scatter_dimension=0, tiled=True)
    aggregate = summed.astype(jnp.bfloat16)
    pre_act = jnp.dot(aggregate, weight, preferred_element_type=jnp.float32)
    sigma = jax.nn.sigmoid(pre_act)
    activations = (pre_act * sigma).astype(jnp.bfloat16)
    grad_pre = (cotangent.astype(jnp.float32) * sigma * (1.0 + pre_act * (1.0 - sigma))).astype(
        jnp.bfloat16
    )
    weight_terms = jnp.dot(aggregate.T, grad_pre, preferred_element_type=jnp.float32)
    share = lax.psum_scatter(
        weight_terms.astype(jnp.bfloat16), ("col", "rep"), scatter_dimension=0, tiled=True
    ).astype(jnp.float32)
    share = lax.psum(share, "row")
    weight_grad = lax.all_gather(share, ("col", "rep"), axis=0, tiled=True)
    back_rows = jnp.dot(grad_pre, weight.T, preferred_element_type=jnp.float32).astype(jnp.bfloat16)
    back_all = lax.all_gather(back_rows, ("col", "rep"), axis=0, tiled=True)
    back_blocks = back_all.reshape(row_blocks, 128, back_all.shape[1])

    def backward_step(total, piece):
        blocks_g, rows_g, cols_g, live_g = piece
        chosen = back_blocks[rows_g]
        product = jnp.einsum("bji,bjf->bif", blocks_g, chosen, preferred_element_type=jnp.float32)
        return (total.at[cols_g].add(product * live_g[:, None, None]), None)

    grad_terms, _ = lax.scan(
        backward_step, jnp.zeros((col_blocks, 128, back_all.shape[1]), jnp.float32), pieces
    )
    grad_terms = grad_terms.reshape(col_blocks * 128, back_all.shape[1])
    input_grad = lax.psum_scatter(
        grad_terms.astype(jnp.bfloat16), "row", scatter_dimension=1, tiled=True
    )
    return (activations, input_grad, weight_grad)


def solution(mesh):
    in_specs = (
        P(("col", "rep"), "row"),
        P(),
        P(("row", "col", "rep"), None),
        P("row", ("col", "rep"), None, None, None),
        P("row", ("col", "rep"), None, None),
        P("row", ("col", "rep")),
    )
    out_specs = (P(("row", "col", "rep"), None), P(("col", "rep"), "row"), P())
    return jax.shard_map(local, mesh=mesh, in_specs=in_specs, out_specs=out_specs, check_vma=False)
```

profile of v0, /device:TPU:0, one launch (start us, length us, event | category | flops | bytes accessed | tf_op | source)
XLA Modules:
  0.0 228.0 jit_solution(13461801693741192329)
XLA Ops:
  7.2 0.8 slice_reduce_fusion
  8.0 0.1 reshape_squeeze.11
  8.1 0.1 reshape_squeeze.9
  8.8 17.6 %all_gather.9 = bf16[1024,256]{0,1:T(8,128)(2,1)S(1)} all-gather(bf16[1024,64]{0,1:T(8,128)(2,1)} %param.10), channel_id=1, replica_groups=mesh['row'=4,'col'=2,'rep'=4] {'row'}, dimensions={1}, use_global_device_ids=true | all-gather | bytes 655360 | tf_op jit(solution)/shard_map/all_gather | solution.py:14
  26.4 0.2 copy.10
  26.6 0.2 broadcast_in_dim.4
  26.8 45.1 %while.20 = (s32[]{:T(128)}, f32[16,128,256]{2,1,0:T(8,128)S(1)}, s32[2,64]{1,0:T(2,128)S(1)}, bf16[2,64,128,128]{3,2,1,0:T(8,128)(2,1)}, s32[2,64]{1,0:T(2,128)...) while((s32[]{:T(128)}, f32[16,128,256]{2,1,0:T(8,128)S(1)}, ...), condition=%wide.region_2.3_spmd, body=%wide.region_0.2_spmd.sunk | while | flops 541066624 | bytes 48241756 | solution.py:35
  26.9 2.8 %gather_fusion = bf16[64,128,256]{2,1,0:T(8,128)(2,1)} fusion(bf16[8,128,256]{2,1,0:T(8,128)(2,1)S(1)} %get-tuple-element.237, s32[1024]{0:T(1024)S(1)} %pad_clamp_fusion.4), kind=kCustom, calls=%fused_computation.clone.1 | custom fusion | bytes 8388864 | tf_op jit(solution)/shard_map/while/body/eval_jaxpr/gather | solution.py:31
  29.7 7.3 %broadcast_multiply_fusion.4 = f32[64,128,256]{2,1,0:T(8,128)} fusion(f32[64]{0:T(128)S(1)} %fusion.36, bf16[64,128,256]{2,1,0:T(8,128)(2,1)} %gather_fusion, bf16[2,64,128,128]{3,2,1,0:T(8,128)(2,1)} %get-tuple-element.235, s32[]{:T(128)} %get-tuple-element.224), kind=kOutput, calls=%fused_computation.4.clone.1 | convolution fusion | flops 538968064 | bytes 14680832 | tf_op jit(solution)/shard_map/while/body/eval_jaxpr/bij,bjf->bif/dot_general | solution.py:32
  37.0 12.4 %scatter_fusion = f32[16,128,256]{2,1,0:T(8,128)S(1)} fusion(f32[16,128,256]{2,1,0:T(8,128)S(1)} %get-tuple-element.225, s32[64]{0:T(128)S(1)} %get-tuple-element.205, f32[64,128,256]{2,1,0:T(8,128)} %broadcast_multiply_fusion.4), kind=kCustom, calls=%fused_computation.2.clone.1 | custom fusion | flops 2097152 | bytes 25166080 | tf_op jit(solution)/shard_map/while/body/eval_jaxpr/scatter-add | solution.py:33
  49.4 2.8 %gather_fusion = bf16[64,128,256]{2,1,0:T(8,128)(2,1)} fusion(bf16[8,128,256]{2,1,0:T(8,128)(2,1)S(1)} %get-tuple-element.237, s32[1024]{0:T(1024)S(1)} %pad_clamp_fusion.4), kind=kCustom, calls=%fused_computation.clone.1 | custom fusion | bytes 8388864 | tf_op jit(solution)/shard_map/while/body/eval_jaxpr/gather | solution.py:31
  52.2 7.3 %broadcast_multiply_fusion.4 = f32[64,128,256]{2,1,0:T(8,128)} fusion(f32[64]{0:T(128)S(1)} %fusion.36, bf16[64,128,256]{2,1,0:T(8,128)(2,1)} %gather_fusion, bf16[2,64,128,128]{3,2,1,0:T(8,128)(2,1)} %get-tuple-element.235, s32[]{:T(128)} %get-tuple-element.224), kind=kOutput, calls=%fused_computation.4.clone.1 | convolution fusion | flops 538968064 | bytes 14680832 | tf_op jit(solution)/shard_map/while/body/eval_jaxpr/bij,bjf->bif/dot_general | solution.py:32
  59.5 12.4 %scatter_fusion = f32[16,128,256]{2,1,0:T(8,128)S(1)} fusion(f32[16,128,256]{2,1,0:T(8,128)S(1)} %get-tuple-element.225, s32[64]{0:T(128)S(1)} %get-tuple-element.205, f32[64,128,256]{2,1,0:T(8,128)} %broadcast_multiply_fusion.4), kind=kCustom, calls=%fused_computation.2.clone.1 | custom fusion | flops 2097152 | bytes 25166080 | tf_op jit(solution)/shard_map/while/body/eval_jaxpr/scatter-add | solution.py:33
  72.0 1.3 copy-done.1
  73.4 43.0 %reduce-scatter.4.cloned.1.call-done = f32[256,256]{1,0:T(8,128)} async-done(((f32[2048,256]{1,0:T(8,128)}), f32[256,256]{1,0:T(8,128)}) %reduce-scatter.4.cloned.1.call-update) | async-done | bytes 262160 | tf_op jit(solution)/shard_map/reduce_scatter | solution.py:39
  116.4 1.9 multiply_convert_fusion
  118.2 0.9 convolution_convert_fusion.1
  119.2 6.4 %copy.9 = bf16[1,1,128,128,128]{3,4,2,1,0:T(8,128)(2,1)} copy(bf16[1,1,128,128,128]{4,3,2,1,0:T(8,128)(2,1)} %bitcast.81) | data formatting | bytes 8388608 | tf_op args[3]
  125.6 0.9 convolution_convert_fusion
  126.6 16.1 %all-gather.2.cloned.1.call-done = bf16[2048,256]{1,0:T(8,128)(2,1)} async-done(((bf16[256,256]{1,0:T(8,128)(2,1)}), bf16[2048,256]{1,0:T(8,128)(2,1)}) %all-gather.2.cloned.1.call-update) | async-done | bytes 1048592 | tf_op jit(solution)/shard_map/all_gather | solution.py:54
  142.7 0.1 broadcast_in_dim.8
  142.8 47.5 %while.21 = (s32[]{:T(128)}, f32[8,128,256]{2,1,0:T(8,128)S(1)}, s32[2,64]{1,0:T(2,128)S(1)}, bf16[2,64,128,128]{2,3,1,0:T(8,128)(2,1)}, s32[2,64]{1,0:T(2,128)S...) while((s32[]{:T(128)}, f32[8,128,256]{2,1,0:T(8,128)S(1)}, s32[2,64]{1,0:T(2,128)S(1)}, ...), condition=%wide.region_6.7_spmd, body=%wide.region_4.6_spmd.sunk | while | flops 541066624 | bytes 48241756 | solution.py:63
  142.8 4.0 %gather_fusion.1 = bf16[64,128,256]{2,1,0:T(8,128)(2,1)} fusion(bf16[16,128,256]{2,1,0:T(8,128)(2,1)} %get-tuple-element.261, s32[1024]{0:T(1024)S(1)} %pad_clamp_fusion.5), kind=kCustom, calls=%fused_computation.1.clone.1 | custom fusion | bytes 8388864 | tf_op jit(solution)/shard_map/while/body/eval_jaxpr/gather | solution.py:59
  146.8 7.3 %broadcast_multiply_fusion.5 = f32[64,128,256]{2,1,0:T(8,128)} fusion(f32[64]{0:T(128)S(1)} %fusion.40, bf16[64,128,256]{2,1,0:T(8,128)(2,1)} %gather_fusion.1, bf16[2,64,128,128]{2,3,1,0:T(8,128)(2,1)} %get-tuple-element.259, s32[]{:T(128)} %get-tuple-element.248), kind=kOutput, calls=%fused_computation.19.clone.1 | convolution fusion | flops 538968064 | bytes 14680832 | tf_op jit(solution)/shard_map/while/body/eval_jaxpr/bji,bjf->bif/dot_general | solution.py:60
  154.1 12.4 %scatter_fusion.1 = f32[8,128,256]{2,1,0:T(8,128)S(1)} fusion(f32[8,128,256]{2,1,0:T(8,128)S(1)} %get-tuple-element.249, s32[64]{0:T(128)S(1)} %get-tuple-element.214, f32[64,128,256]{2,1,0:T(8,128)} %broadcast_multiply_fusion.5), kind=kCustom, calls=%fused_computation.3.clone.1 | custom fusion | flops 2097152 | bytes 25166080 | tf_op jit(solution)/shard_map/while/body/eval_jaxpr/scatter-add | solution.py:61
  166.5 4.0 %gather_fusion.1 = bf16[64,128,256]{2,1,0:T(8,128)(2,1)} fusion(bf16[16,128,256]{2,1,0:T(8,128)(2,1)} %get-tuple-element.261, s32[1024]{0:T(1024)S(1)} %pad_clamp_fusion.5), kind=kCustom, calls=%fused_computation.1.clone.1 | custom fusion | bytes 8388864 | tf_op jit(solution)/shard_map/while/body/eval_jaxpr/gather | solution.py:59
  170.5 7.3 %broadcast_multiply_fusion.5 = f32[64,128,256]{2,1,0:T(8,128)} fusion(f32[64]{0:T(128)S(1)} %fusion.40, bf16[64,128,256]{2,1,0:T(8,128)(2,1)} %gather_fusion.1, bf16[2,64,128,128]{2,3,1,0:T(8,128)(2,1)} %get-tuple-element.259, s32[]{:T(128)} %get-tuple-element.248), kind=kOutput, calls=%fused_computation.19.clone.1 | convolution fusion | flops 538968064 | bytes 14680832 | tf_op jit(solution)/shard_map/while/body/eval_jaxpr/bji,bjf->bif/dot_general | solution.py:60
  177.8 12.4 %scatter_fusion.1 = f32[8,128,256]{2,1,0:T(8,128)S(1)} fusion(f32[8,128,256]{2,1,0:T(8,128)S(1)} %get-tuple-element.249, s32[64]{0:T(128)S(1)} %get-tuple-element.214, f32[64,128,256]{2,1,0:T(8,128)} %broadcast_multiply_fusion.5), kind=kCustom, calls=%fused_computation.3.clone.1 | custom fusion | flops 2097152 | bytes 25166080 | tf_op jit(solution)/shard_map/while/body/eval_jaxpr/scatter-add | solution.py:61
  190.3 1.0 copy.14
  191.3 20.2 %psum.7 = f32[32,256]{1,0:T(8,128)S(1)} all-reduce(bf16[32,256]{1,0:T(8,128)(2,1)} %reduce-scatter.8.cloned.1.call-done), channel_id=1, replica_groups=mesh['row'=4,'col'=2,'rep'=4] {'row'}, use_global_device_ids=true, to_apply=%region_9.10 | all-reduce | flops 8192 | bytes 49152 | tf_op jit(solution)/shard_map/psum | solution.py:51
  211.6 9.2 %all_gather.11 = f32[256,256]{1,0:T(8,128)S(1)} all-gather(f32[32,256]{1,0:T(8,128)S(1)} %psum.7), channel_id=1, replica_groups=mesh['row'=4,'col'=2,'rep'=4] {'col','rep'}, dimensions={0}, use_global_device_ids=true | all-gather | bytes 294912 | tf_op jit(solution)/shard_map/all_gather | solution.py:52
  220.8 0.7 copy.33
  (31 shorter events, 0.4 us)
Async XLA Ops:
  7.2 109.2 %copy-start = (bf16[256,256]{1,0:T(8,128)(2,1)S(1)}, bf16[256,256]{1,0:T(8,128)(2,1)}, u32[]{:S(2)}) copy-start(bf16[256,256]{1,0:T(8,128)(2,1)} %param.11) | copy-start | bytes 393220
  7.2 109.2 %reduce-scatter.4.cloned.1.call-start = ((), (), s32[]{:S(2)}) async-start(), calls=%async_computation.3 | async-start | bytes 2359296 | tf_op jit(solution)/shard_map/reduce_scatter | solution.py:39
  26.8 89.5 %copy-start.3 = (bf16[256,256]{1,0:T(8,128)(2,1)S(1)}, bf16[256,256]{1,0:T(8,128)(2,1)}, u32[]{:S(2)}) copy-start(bf16[256,256]{1,0:T(8,128)(2,1)} %param.12) | copy-start | bytes 393220
  72.0 1.4 copy-start.1
  73.3 69.3 %all-gather.2.cloned.1.call-start = ((), (), s32[]{:S(2)}) async-start(), calls=%async_computation.4 | async-start | bytes 1179648 | tf_op jit(solution)/shard_map/all_gather | solution.py:54
  119.1 6.5 %copy-start.2 = (f32[256,256]{1,0:T(8,128)S(1)}, f32[256,256]{1,0:T(8,128)}, u32[]{:S(2)}) copy-start(f32[256,256]{1,0:T(8,128)} %reduce-scatter.4.cloned.1.call-done) | copy-start | bytes 786436
  119.2 72.2 %reduce-scatter.8.cloned.1.call-start = ((), (), s32[]{:S(2)}) async-start(), calls=%async_computation.6 | async-start | bytes 147456 | tf_op jit(solution)/shard_map/reduce_scatter | solution.py:48
  126.5 94.3 %reduce-scatter.6.cloned.1.call-start = ((), (), s32[]{:S(2)}) async-start(), calls=%async_computation.5 | async-start | bytes 655360 | tf_op jit(solution)/shard_map/reduce_scatter | solution.py:67
Sparse Core Ops, SparseCore 0:
  73.5 42.8 reduce-scatter.3
  119.3 23.3 all-gather.1
  146.3 33.5 reduce-scatter.7
  191.4 22.1 reduce-scatter.5
where the time goes:
time: 229 us; the launch traced here: 228 us
  waiting for transfers between devices  59.2 us (26%)
  other arithmetic  49.7 us (22%)
  blocking collectives  47 us (21%)
  matrix products  32.8 us (14%)
  local copies, waits for them, and re-layouts  24.5 us (11%)
  between operations  14.5 us (6%)
    reduce_scatter x1, waiting for transfers between devices, local(): lax.psum_scatter(partial_value, ('col', 'rep'), scatter_dimension=0, tile...  43 us
    scatter-add x2, other arithmetic, forward_step(): return (total.at[rows_g].add(product * live_g[:, None, None]), None)  24.9 us
    scatter-add x2, other arithmetic, backward_step(): return (total.at[cols_g].add(product * live_g[:, None, None]), None)  24.8 us
    psum x1, blocking collectives, local(): share = lax.psum(share, 'row')  20.2 us
    all_gather x1, blocking collectives, local(): gathered = lax.all_gather(features, 'row', axis=1, tiled=True)  17.6 us
    all_gather x1, waiting for transfers between devices, local(): back_all = lax.all_gather(back_rows, ('col', 'rep'), axis=0, tiled=True)  16.1 us
    dot_general x2, matrix products, backward_step(): jnp.einsum('bji,bjf->bif', blocks_g, chosen, preferred_element_type=jnp.f...  14.6 us
    dot_general x2, matrix products, forward_step(): jnp.einsum('bij,bjf->bif', blocks_g, chosen, preferred_element_type=jnp.f...  14.6 us
  transfers between devices with their start and end apart: 4, of which 2 were waited for; matrix products, arithmetic and copies ran while one was open for 24% of the time, Pallas kernels for 0%

commit v1 on v0

--- a/solution.py
+++ b/solution.py
@@ -1,12 +1,15 @@
+import functools
 import math
 
 import jax
 import jax.numpy as jnp
 from jax import lax
+from jax.experimental import pallas as pl
+from jax.experimental.pallas import tpu as pltpu
 from jax.sharding import PartitionSpec as P
 
 
-def local(features, weight, cotangent, block_values, block_coords, block_counts):
+def local_xla(features, weight, cotangent, block_values, block_coords, block_counts):
     blocks = block_values[0, 0]
     coords = block_coords[0, 0]
     live_count = block_counts[0, 0]
@@ -70,6 +73,362 @@
     return (activations, input_grad, weight_grad)
 
 
+BF16 = jnp.bfloat16
+F32 = jnp.float32
+VMEM_BUDGET = 60 * 2**20
+MESH = pl.DeviceIdType.MESH
+
+
+def dot(a, b, ca=1, cb=0):
+    return lax.dot_general(a, b, (((ca,), (cb,)), ((), ())), preferred_element_type=F32)
+
+
+def layer_kernel(
+    sizes,
+    table,
+    feat_in,
+    weight_in,
+    cot_in,
+    blocks_hbm,
+    act_out,
+    igrad_out,
+    wgrad_out,
+    fbuf,
+    bbuf,
+    sums,
+    dense,
+    feat,
+    pbuf,
+    prec,
+    qbuf,
+    qrec,
+    own_back,
+    brec,
+    bpar,
+    total,
+    zbuf,
+    zrec,
+    wbuf,
+    wrec,
+    shard_buf,
+    srec,
+    wall,
+    wgather,
+    load_sem,
+    f_sem,
+    p_sem,
+    q_sem,
+    b_sem,
+    c_sem,
+    z_sem,
+    w_sem,
+    s_sem,
+    g_sem,
+    h_sem,
+):
+    nrow, ncol, nrep = sizes
+    nh = nrep // 2
+    group = ncol * nrep
+    slots = bbuf.shape[0]
+    nodes, width = act_out.shape
+    fw = feat_in.shape[1]
+    col_nodes = feat_in.shape[0]
+    row_blocks, col_blocks = dense.shape[0] // 128, dense.shape[1] // 128
+    r, c, p = lax.axis_index("row"), lax.axis_index("col"), lax.axis_index("rep")
+    h, k = p // 2, p % 2
+    g = c * nrep + p
+    partner = h * 2 + (1 - k)
+    offsets = [(dc, dh) for dc in reversed(range(ncol)) for dh in reversed(range(nh))]
+    chips = len(offsets)
+
+    def to_row(j):
+        return {"row": (r + j) % nrow}
+
+    def to_group(j):
+        q = (g + j) % group
+        return {"col": q // nrep, "rep": q % nrep}
+
+    def to_chip(i):
+        dc, dh = offsets[i]
+        return {"col": (c + dc) % ncol, "rep": ((h + dh) % nh) * 2 + k}
+
+    def part_to(i, core):
+        dc, dh = offsets[i]
+        return ((c + dc) % ncol) * nrep + ((h + dh) % nh) * 2 + core
+
+    def part_from(i, core):
+        dc, dh = offsets[i]
+        return ((c + ncol - dc) % ncol) * nrep + ((h + nh - dh) % nh) * 2 + core
+
+    def rcopy(src, dst, sems, i, device):
+        return pltpu.make_async_remote_copy(
+            src_ref=src,
+            dst_ref=dst,
+            send_sem=sems.at[0, i],
+            recv_sem=sems.at[1, i],
+            device_id=device,
+            device_id_type=MESH,
+        )
+
+    chunks = load_sem.shape[0]
+    per = slots // chunks
+    loads = []
+    for i in range(chunks):
+        span = pl.ds(i * per, per)
+        loads.append(pltpu.make_async_copy(blocks_hbm.at[span], bbuf.at[span], load_sem.at[i]))
+        loads[-1].start()
+
+    barrier = pltpu.get_barrier_semaphore()
+    for j in range(1, nrow):
+        pl.semaphore_signal(barrier, inc=1, device_id=to_row(j), device_id_type=MESH)
+    for j in range(1, group):
+        pl.semaphore_signal(barrier, inc=1, device_id=to_group(j), device_id_type=MESH)
+
+    packs = 128 // fw
+    piece = col_nodes // packs
+    packed = jnp.concatenate(
+        [feat_in[i * piece : (i + 1) * piece, :] for i in range(packs)], axis=1
+    )
+    fbuf[r] = packed
+    pl.semaphore_wait(barrier, nrow - 1 + group - 1)
+    fcopies = []
+    for j in range(1, nrow):
+        fcopies.append(rcopy(fbuf.at[r], fbuf.at[r], f_sem, j - 1, to_row(j)))
+        fcopies[-1].start()
+
+    sums[0] = jnp.zeros((128, 128), F32)
+    for i in range(chunks):
+        loads[i].wait()
+
+        def add_slot(s, carry):
+            sums[s + 1] = sums[table[s]] + bbuf[s].astype(F32)
+            return carry
+
+        lax.fori_loop(i * per, (i + 1) * per, add_slot, 0)
+
+    def fill(rb, carry):
+        for cb in range(col_blocks):
+            block = sums[table[slots + rb * col_blocks + cb]]
+            dense[pl.ds(rb * 128, 128), cb * 128 : (cb + 1) * 128] = block.astype(BF16)
+        return carry
+
+    lax.fori_loop(0, row_blocks, fill, 0)
+
+    for copy in fcopies:
+        copy.wait()
+    for q in range(packs):
+        for m in range(width // 128):
+            feat[q * piece : (q + 1) * piece, m * 128 : (m + 1) * 128] = jnp.concatenate(
+                [fbuf[m * packs + e, :, q * fw : (q + 1) * fw] for e in range(packs)], axis=1
+            )
+
+    def partial(part):
+        return dot(dense[pl.ds(part * nodes, nodes), :], feat[...])
+
+    pcopies = []
+    for i in range(chips):
+        pbuf[i] = partial(part_to(i, 1 - k)).astype(BF16)
+        pcopies.append(rcopy(pbuf.at[i], prec.at[i], p_sem, i, {"rep": partner}))
+        pcopies[i].start()
+    qcopies = []
+    for i in range(chips - 1):
+        mine = partial(part_to(i, k))
+        pcopies[i].wait()
+        qbuf[i] = (mine + prec[i].astype(F32)).astype(BF16)
+        qcopies.append(rcopy(qbuf.at[i], qrec.at[i], q_sem, i, to_chip(i)))
+        qcopies[i].start()
+    summed = partial(g)
+    pcopies[chips - 1].wait()
+    summed = summed + prec[chips - 1].astype(F32)
+    for i in reversed(range(chips - 1)):
+        qcopies[i].wait()
+        summed = summed + qrec[i].astype(F32)
+
+    aggregate = summed.astype(BF16)
+    pre_act = dot(aggregate, weight_in[...])
+    sigma = jax.nn.sigmoid(pre_act)
+    grad_pre = (cot_in[...].astype(F32) * sigma * (1.0 + pre_act * (1.0 - sigma))).astype(BF16)
+    own_back[...] = dot(weight_in[...], grad_pre, 1, 1).astype(BF16)
+    bcopies, ccopies = [], []
+    for i in range(chips - 1):
+        bcopies.append(rcopy(own_back, brec.at[i], b_sem, i, to_chip(i)))
+        bcopies[i].start()
+    first = rcopy(own_back, bpar.at[chips - 1], c_sem, chips - 1, {"rep": partner})
+    first.start()
+
+    terms = dot(aggregate, grad_pre, 0, 0)
+    wrows = width // nrow
+    wbuf[...] = terms.astype(BF16).reshape(nrow, wrows, width)
+    wcopies = []
+    for j in range(1, nrow):
+        wcopies.append(rcopy(wbuf.at[(r + j) % nrow], wrec.at[j - 1], w_sem, j - 1, to_row(j)))
+        wcopies[-1].start()
+    act_out[...] = (pre_act * sigma).astype(BF16)
+
+    def back_term(piece_t, part):
+        return dot(piece_t, dense[pl.ds(part * nodes, nodes), :])
+
+    total[...] = back_term(own_back[...], g)
+    first.wait()
+    total[...] += back_term(bpar[chips - 1], c * nrep + partner)
+
+    for copy in wcopies:
+        copy.wait()
+    share = wbuf[r].astype(F32)
+    for j in range(nrow - 1):
+        share = share + wrec[j].astype(F32)
+    srows = wrows // group
+    shard_buf[...] = share.reshape(group, srows, width)
+    scopies = []
+    for j in range(1, group):
+        scopies.append(rcopy(shard_buf.at[(g + j) % group], srec.at[j - 1], s_sem, j - 1, to_group(j)))
+        scopies[-1].start()
+
+    for i in reversed(range(chips - 1)):
+        bcopies[i].wait()
+        ccopies.append(rcopy(brec.at[i], bpar.at[i], c_sem, i, {"rep": partner}))
+        ccopies[-1].start()
+        total[...] += back_term(brec[i], part_from(i, k))
+
+    for copy in scopies:
+        copy.wait()
+    final = shard_buf[g]
+    for j in range(group - 1):
+        final = final + srec[j]
+    wall[g] = final
+    gcopies = []
+    for j in range(1, group):
+        gcopies.append(rcopy(wall.at[g], wall.at[g], g_sem, j - 1, to_group(j)))
+        gcopies[-1].start()
+
+    for n, i in enumerate(reversed(range(chips - 1))):
+        ccopies[n].wait()
+        total[...] += back_term(bpar[i], part_from(i, 1 - k))
+
+    zcopies = []
+    for j in range(1, nrow):
+        q = (r + j) % nrow
+        zbuf[j - 1] = total[pl.ds(q * fw, fw), :].astype(BF16)
+        zcopies.append(rcopy(zbuf.at[j - 1], zrec.at[j - 1], z_sem, j - 1, to_row(j)))
+        zcopies[-1].start()
+
+    for copy in gcopies:
+        copy.wait()
+    wgather[r] = wall[...].reshape(wrows, width)
+    hcopies = []
+    for j in range(1, nrow):
+        hcopies.append(rcopy(wgather.at[r], wgather.at[r], h_sem, j - 1, to_row(j)))
+        hcopies[-1].start()
+
+    mine = total[pl.ds(r * fw, fw), :]
+    for j in range(nrow - 1):
+        zcopies[j].wait()
+        mine = mine + zrec[j].astype(F32)
+    stacked = jnp.concatenate(
+        [mine[:, i * piece : (i + 1) * piece] for i in range(packs)], axis=0
+    ).T
+    for i in range(packs):
+        igrad_out[i * piece : (i + 1) * piece, :] = stacked[:, i * fw : (i + 1) * fw].astype(BF16)
+    for copy in hcopies:
+        copy.wait()
+    wgrad_out[...] = wgather[...].reshape(width, width)
+
+
+def local_kernel(sizes, features, weight, cotangent, block_values, block_coords, block_counts):
+    nrow, ncol, nrep = sizes
+    group = ncol * nrep
+    chips = group // 2
+    blocks = block_values[0, 0]
+    coords = block_coords[0, 0]
+    live_count = block_counts[0, 0]
+    slots = blocks.shape[0]
+    nodes, width = cotangent.shape
+    col_nodes, fw = features.shape
+    row_blocks, col_blocks = nodes * group // 128, col_nodes // 128
+    places = row_blocks * col_blocks
+    place = coords[:, 0] * col_blocks + coords[:, 1]
+    slot = jnp.arange(slots, dtype=jnp.int32)
+    wanted = jnp.concatenate([place, jnp.arange(places, dtype=jnp.int32)])
+    limit = jnp.concatenate([slot, jnp.full((places,), slots, jnp.int32)])
+    hit = (wanted[:, None] == place[None, :]) & (
+        slot[None, :] < jnp.minimum(limit, live_count)[:, None]
+    )
+    table = jnp.max(jnp.where(hit, slot[None, :] + 1, 0), axis=1)
+
+    packs = 128 // fw
+    chunks = math.gcd(slots, 8)
+    wrows = width // nrow
+    srows = wrows // group
+    square = (nodes, width)
+    vmem = functools.partial(pl.BlockSpec, memory_space=pltpu.VMEM)
+    dma = pltpu.SemaphoreType.DMA
+    return pl.pallas_call(
+        functools.partial(layer_kernel, sizes),
+        out_shape=(
+            jax.ShapeDtypeStruct(square, BF16),
+            jax.ShapeDtypeStruct((col_nodes, fw), BF16),
+            jax.ShapeDtypeStruct((width, width), F32),
+        ),
+        in_specs=[
+            pl.BlockSpec(memory_space=pltpu.SMEM),
+            vmem(),
+            vmem(),
+            vmem(),
+            pl.BlockSpec(memory_space=pl.ANY),
+        ],
+        out_specs=(vmem(), vmem(), vmem()),
+        scratch_shapes=[
+            pltpu.VMEM((nrow, col_nodes // packs, 128), BF16),
+            pltpu.VMEM((slots, 128, 128), BF16),
+            pltpu.VMEM((slots + 1, 128, 128), F32),
+            pltpu.VMEM((row_blocks * 128, col_nodes), BF16),
+            pltpu.VMEM((col_nodes, width), BF16),
+            pltpu.VMEM((chips,) + square, BF16),
+            pltpu.VMEM((chips,) + square, BF16),
+            pltpu.VMEM((chips - 1,) + square, BF16),
+            pltpu.VMEM((chips - 1,) + square, BF16),
+            pltpu.VMEM((width, nodes), BF16),
+            pltpu.VMEM((chips - 1, width, nodes), BF16),
+            pltpu.VMEM((chips, width, nodes), BF16),
+            pltpu.VMEM((width, col_nodes), F32),
+            pltpu.VMEM((nrow - 1, fw, col_nodes), BF16),
+            pltpu.VMEM((nrow - 1, fw, col_nodes), BF16),
+            pltpu.VMEM((nrow, wrows, width), BF16),
+            pltpu.VMEM((nrow - 1, wrows, width), BF16),
+            pltpu.VMEM((group, srows, width), F32),
+            pltpu.VMEM((group - 1, srows, width), F32),
+            pltpu.VMEM((group, srows, width), F32),
+            pltpu.VMEM((nrow, wrows, width), F32),
+            dma((chunks,)),
+            dma((2, nrow - 1)),
+            dma((2, chips)),
+            dma((2, chips - 1)),
+            dma((2, chips - 1)),
+            dma((2, chips)),
+            dma((2, nrow - 1)),
+            dma((2, nrow - 1)),
+            dma((2, group - 1)),
+            dma((2, group - 1)),
+            dma((2, nrow - 1)),
+        ],
+        compiler_params=pltpu.CompilerParams(
+            collective_id=0, has_side_effects=True, vmem_limit_bytes=VMEM_BUDGET
+        ),
+    )(table, features, weight, cotangent, blocks)
+
+
+def fits(mesh, features, weight, cotangent, block_values):
+    nrow, ncol, nrep = (mesh.shape[name] for name in ("row", "col", "rep"))
+    group = ncol * nrep
+    width = features.shape[1]
+    fw = width // nrow
+    rows, cols = cotangent.shape[0] // nrow, features.shape[0] // group
+    tile = rows * cols * 2 + block_values.shape[2] * 128 * 128 * 6
+    moved = 8 * rows * width + 12 * cols * width
+    whole = nrep % 2 == 0 and 128 % fw == 0 and (width // nrow) % (8 * group) == 0
+    return whole and nrow > 1 and group > 2 and tile + moved < VMEM_BUDGET * 3 // 4
+
+
 def solution(mesh):
     in_specs = (
         P(("col", "rep"), "row"),
@@ -80,4 +439,15 @@
         P("row", ("col", "rep")),
     )
     out_specs = (P(("row", "col", "rep"), None), P(("col", "rep"), "row"), P())
-    return jax.shard_map(local, mesh=mesh, in_specs=in_specs, out_specs=out_specs, check_vma=False)
+    sizes = tuple(mesh.shape[name] for name in ("row", "col", "rep"))
+
+    def run(features, weight, cotangent, block_values, block_coords, block_counts):
+        if fits(mesh, features, weight, cotangent, block_values):
+            body = functools.partial(local_kernel, sizes)
+        else:
+            body = local_xla
+        return jax.shard_map(
+            body, mesh=mesh, in_specs=in_specs, out_specs=out_specs, check_vma=False
+        )(features, weight, cotangent, block_values, block_coords, block_counts)
+
+    return run

time: 229 us -> 68.6 us (0.30)
  waiting for transfers between devices: 59.2 us -> 0 us
  Pallas kernels: 0 us -> 58 us
  other arithmetic: 49.7 us -> 2.23 us
  blocking collectives: 47 us -> 0 us
  matrix products: 32.8 us -> 0 us
  local copies, waits for them, and re-layouts: 24.5 us -> 6.71 us
  between operations: 14.5 us -> 1.29 us
    pallas_call x0 -> x1, Pallas kernels: none -> 58 us  [local_kernel(): pl.pallas_call(functools.partial(layer_kernel, sizes), out_shape=(jax.Sha...]
    scatter-add x4 -> x0, other arithmetic: 49.6 us -> none  [the longest x2 24.9 us: forward_step(): return (total.at[rows_g].add(product * live_g[:, None, None]), None)]
    reduce_scatter x3 -> x0, waiting for transfers between devices: 43 us -> none  [the longest x1 43 us: local(): lax.psum_scatter(partial_value, ('col', 'rep'), scatter_dimension=0, tile...]
    dot_general x7 -> x0, matrix products: 32.8 us -> none  [the longest x2 14.6 us: backward_step(): jnp.einsum('bji,bjf->bif', blocks_g, chosen, preferred_element_type=jnp.f...]
    all_gather x2 -> x0, blocking collectives: 26.8 us -> none  [the longest x1 17.6 us: local(): gathered = lax.all_gather(features, 'row', axis=1, tiled=True)]
    psum x1 -> x0, blocking collectives: 20.2 us -> none  [local(): share = lax.psum(share, 'row')]
    all_gather x1 -> x0, waiting for transfers between devices: 16.1 us -> none  [local(): back_all = lax.all_gather(back_rows, ('col', 'rep'), axis=0, tiled=True)]
    gather x4 -> x0, local copies, waits for them, and re-layouts: 13.6 us -> none  [the longest x2 8 us: backward_step(): chosen = back_blocks[rows_g]]
  transfers between devices with their start and end apart: 4 -> 0, of which waited for: 2 -> 0; matrix products, arithmetic and copies ran while one was open for 24% -> 0% of each run, Pallas kernels for 0% -> 0%
where the time goes in v1:
time: 68.6 us; the launch traced here: 68.3 us
  Pallas kernels  58 us (85%)
  local copies, waits for them, and re-layouts  6.71 us (10%)
  other arithmetic  2.23 us (3%)
  between operations  1.29 us (2%)
    pallas_call x1, Pallas kernels, local_kernel(): pl.pallas_call(functools.partial(layer_kernel, sizes), out_shape=(jax.Sha...  58 us
    unnamed x3, local copies, waits for them, and re-layouts  4.98 us
    pallas_call x1, local copies, waits for them, and re-layouts, local_kernel(): pl.pallas_call(functools.partial(layer_kernel, sizes), out_shape=(jax.Sha...  1.73 us

profile of v1, /device:TPU:0, one launch (start us, length us, event | category | flops | bytes accessed | tf_op | source)
XLA Modules:
  0.0 68.3 jit_solution(6660459175673406146)
XLA Ops:
  1.3 0.8 %add_bitcast_fusion = s32[128]{0:T(128)S(1)} fusion(s32[128,2]{0,1:T(2,128)} %bitcast.7), kind=kLoop, calls=%fused_computation.6 | loop fusion | flops 256 | bytes 1536 | tf_op jit(solution)/shard_map/add | solution.py:349
  2.0 0.7 %pad_add_fusion = (s32[256]{0:T(256)S(1)}, s32[256]{0:T(256)S(1)}) fusion(s32[128]{0:T(128)S(1)} %iota.10, s32[128]{0:T(128)S(1)} %add_bitcast_fusion, s32[256]{0:T(256)} %constant.2.clone.1, s32[]{:T(128)} %bitcast.5), kind=kLoop, calls=%fused_computation.3 | loop fusion | flops 512 | bytes 4100 | tf_op jit(solution)/shard_map/concatenate | solution.py:351
  2.7 0.8 %select_reduce_fusion.table = s32[256]{0:T(256)} fusion(s32[128]{0:T(128)S(1)} %iota_add_fusion, s32[256]{0:T(256)S(1)} %get-tuple-element.10, s32[128]{0:T(128)S(1)} %add_bitcast_fusion, s32[256]{0:T(256)S(1)} %get-tuple-element.9), kind=kLoop, calls=%fused_computation | loop fusion | flops 163584 | bytes 4096 | tf_op jit(solution)/shard_map/reduce_max | solution.py:356
  3.5 1.7 %copy.11.feat_in = bf16[1024,64]{1,0:T(8,128)(2,1)} copy(bf16[1024,64]{0,1:T(8,128)(2,1)} %param.6) | data formatting | bytes 262144 | tf_op args[0]
  5.3 58.0 %shard_map.85 = (bf16[256,256]{1,0:T(8,128)(2,1)}, bf16[1024,64]{1,0:T(8,128)(2,1)}, f32[256,256]{1,0:T(8,128)}) custom-call(s32[256]{0:T(256)} %select_reduce_fusion.table, bf16[1024,64]{1,0:T(8,128)(2,1)} %copy.11.feat_in, bf16[256,256]{1,0:T(8,128)(2,1)} %weight_in.1, bf16[256,256]{1,0:T(8,128)(2,1)} %cot_in.1, bf16[128,128,128]{2,1,0:T(8,128)(2,1)} %bitcast.6), custom_call_target="tpu_custom_call" | custom-call | tf_op jit(solution)/shard_map/pallas_call | solution.py:365
  63.3 1.7 %copy.12 = bf16[1024,64]{0,1:T(8,128)(2,1)} copy(bf16[1024,64]{1,0:T(8,128)(2,1)} %get-tuple-element.7) | data formatting | bytes 262144 | tf_op jit(solution)/shard_map/pallas_call | solution.py:365
  65.0 1.6 %copy.16 = bf16[256,256]{1,0:T(8,128)(2,1)} copy(bf16[256,256]{1,0:T(8,128)(2,1)} %get-tuple-element.14) | data formatting | bytes 262144
  66.6 1.7 %copy.17 = f32[256,256]{1,0:T(8,128)} copy(f32[256,256]{1,0:T(8,128)} %get-tuple-element.16) | data formatting | bytes 524288
  (2 shorter events, 0.0 us)

commit v2 on v1

--- a/solution.py
+++ b/solution.py
@@ -85,7 +85,8 @@
 
 def layer_kernel(
     sizes,
-    table,
+    count_in,
+    coords_in,
     feat_in,
     weight_in,
     cot_in,
@@ -114,7 +115,10 @@
     srec,
     wall,
     wgather,
+    tvec,
+    table,
     load_sem,
+    t_sem,
     f_sem,
     p_sem,
     q_sem,
@@ -131,8 +135,7 @@
     group = ncol * nrep
     slots = bbuf.shape[0]
     nodes, width = act_out.shape
-    fw = feat_in.shape[1]
-    col_nodes = feat_in.shape[0]
+    fw, col_nodes = feat_in.shape
     row_blocks, col_blocks = dense.shape[0] // 128, dense.shape[1] // 128
     r, c, p = lax.axis_index("row"), lax.axis_index("col"), lax.axis_index("rep")
     h, k = p // 2, p % 2
@@ -184,31 +187,44 @@
     for j in range(1, group):
         pl.semaphore_signal(barrier, inc=1, device_id=to_group(j), device_id_type=MESH)
 
-    packs = 128 // fw
-    piece = col_nodes // packs
-    packed = jnp.concatenate(
-        [feat_in[i * piece : (i + 1) * piece, :] for i in range(packs)], axis=1
-    )
-    fbuf[r] = packed
     pl.semaphore_wait(barrier, nrow - 1 + group - 1)
     fcopies = []
     for j in range(1, nrow):
-        fcopies.append(rcopy(fbuf.at[r], fbuf.at[r], f_sem, j - 1, to_row(j)))
+        fcopies.append(rcopy(feat_in, fbuf.at[r], f_sem, j - 1, to_row(j)))
         fcopies[-1].start()
+
+    fbuf[r] = feat_in[...]
+
+    places = row_blocks * col_blocks
+    live = count_in[0, 0]
+    row_form = coords_in[0:1, :] * col_blocks + coords_in[1:2, :]
+    column_form = jnp.broadcast_to(row_form, (slots, slots)).T
+    mine_at = lax.broadcasted_iota(jnp.int32, (slots, slots), 0)
+    other_at = lax.broadcasted_iota(jnp.int32, (slots, slots), 1)
+    hit = (column_form == row_form) & (mine_at < jnp.minimum(other_at, live))
+    tvec[0:1, 0:slots] = jnp.max(jnp.where(hit, mine_at + 1, 0), axis=0, keepdims=True)
+    for start in range(0, places, slots):
+        hit = (column_form == other_at + start) & (mine_at < live)
+        tvec[0:1, slots + start : 2 * slots + start] = jnp.max(
+            jnp.where(hit, mine_at + 1, 0), axis=0, keepdims=True
+        )
+    tcopy = pltpu.make_async_copy(tvec, table, t_sem)
+    tcopy.start()
+    tcopy.wait()
 
     sums[0] = jnp.zeros((128, 128), F32)
     for i in range(chunks):
         loads[i].wait()
 
         def add_slot(s, carry):
-            sums[s + 1] = sums[table[s]] + bbuf[s].astype(F32)
+            sums[s + 1] = sums[table[0, s]] + bbuf[s].astype(F32)
             return carry
 
         lax.fori_loop(i * per, (i + 1) * per, add_slot, 0)
 
     def fill(rb, carry):
         for cb in range(col_blocks):
-            block = sums[table[slots + rb * col_blocks + cb]]
+            block = sums[table[0, slots + rb * col_blocks + cb]]
             dense[pl.ds(rb * 128, 128), cb * 128 : (cb + 1) * 128] = block.astype(BF16)
         return carry
 
@@ -216,11 +232,7 @@
 
     for copy in fcopies:
         copy.wait()
-    for q in range(packs):
-        for m in range(width // 128):
-            feat[q * piece : (q + 1) * piece, m * 128 : (m + 1) * 128] = jnp.concatenate(
-                [fbuf[m * packs + e, :, q * fw : (q + 1) * fw] for e in range(packs)], axis=1
-            )
+    feat[...] = fbuf[...].reshape(width, col_nodes).T
 
     def partial(part):
         return dot(dense[pl.ds(part * nodes, nodes), :], feat[...])
@@ -324,14 +336,16 @@
     for j in range(nrow - 1):
         zcopies[j].wait()
         mine = mine + zrec[j].astype(F32)
-    stacked = jnp.concatenate(
-        [mine[:, i * piece : (i + 1) * piece] for i in range(packs)], axis=0
-    ).T
-    for i in range(packs):
-        igrad_out[i * piece : (i + 1) * piece, :] = stacked[:, i * fw : (i + 1) * fw].astype(BF16)
+    igrad_out[...] = mine.astype(BF16)
     for copy in hcopies:
         copy.wait()
     wgrad_out[...] = wgather[...].reshape(width, width)
+
+
+def keep_kernel(a_in, b_in, c_in, a_out, b_out, c_out):
+    a_out[...] = a_in[...]
+    b_out[...] = b_in[...]
+    c_out[...] = c_in[...]
 
 
 def local_kernel(sizes, features, weight, cotangent, block_values, block_coords, block_counts):
@@ -339,34 +353,22 @@
     group = ncol * nrep
     chips = group // 2
     blocks = block_values[0, 0]
-    coords = block_coords[0, 0]
-    live_count = block_counts[0, 0]
     slots = blocks.shape[0]
     nodes, width = cotangent.shape
     col_nodes, fw = features.shape
-    row_blocks, col_blocks = nodes * group // 128, col_nodes // 128
-    places = row_blocks * col_blocks
-    place = coords[:, 0] * col_blocks + coords[:, 1]
-    slot = jnp.arange(slots, dtype=jnp.int32)
-    wanted = jnp.concatenate([place, jnp.arange(places, dtype=jnp.int32)])
-    limit = jnp.concatenate([slot, jnp.full((places,), slots, jnp.int32)])
-    hit = (wanted[:, None] == place[None, :]) & (
-        slot[None, :] < jnp.minimum(limit, live_count)[:, None]
-    )
-    table = jnp.max(jnp.where(hit, slot[None, :] + 1, 0), axis=1)
-
-    packs = 128 // fw
+    row_blocks = nodes * group // 128
+    places = row_blocks * (col_nodes // 128)
     chunks = math.gcd(slots, 8)
     wrows = width // nrow
     srows = wrows // group
     square = (nodes, width)
     vmem = functools.partial(pl.BlockSpec, memory_space=pltpu.VMEM)
     dma = pltpu.SemaphoreType.DMA
-    return pl.pallas_call(
+    outs = pl.pallas_call(
         functools.partial(layer_kernel, sizes),
         out_shape=(
             jax.ShapeDtypeStruct(square, BF16),
-            jax.ShapeDtypeStruct((col_nodes, fw), BF16),
+            jax.ShapeDtypeStruct((fw, col_nodes), BF16),
             jax.ShapeDtypeStruct((width, width), F32),
         ),
         in_specs=[
@@ -374,11 +376,12 @@
             vmem(),
             vmem(),
             vmem(),
+            vmem(),
             pl.BlockSpec(memory_space=pl.ANY),
         ],
         out_specs=(vmem(), vmem(), vmem()),
         scratch_shapes=[
-            pltpu.VMEM((nrow, col_nodes // packs, 128), BF16),
+            pltpu.VMEM((nrow, fw, col_nodes), BF16),
             pltpu.VMEM((slots, 128, 128), BF16),
             pltpu.VMEM((slots + 1, 128, 128), F32),
             pltpu.VMEM((row_blocks * 128, col_nodes), BF16),
@@ -399,7 +402,10 @@
             pltpu.VMEM((group - 1, srows, width), F32),
             pltpu.VMEM((group, srows, width), F32),
             pltpu.VMEM((nrow, wrows, width), F32),
+            pltpu.VMEM((1, slots + places), jnp.int32),
+            pltpu.SMEM((1, slots + places), jnp.int32),
             dma((chunks,)),
+            dma,
             dma((2, nrow - 1)),
             dma((2, chips)),
             dma((2, chips - 1)),
@@ -414,7 +420,14 @@
         compiler_params=pltpu.CompilerParams(
             collective_id=0, has_side_effects=True, vmem_limit_bytes=VMEM_BUDGET
         ),
-    )(table, features, weight, cotangent, blocks)
+    )(block_counts, block_coords[0, 0].T, features.T, weight, cotangent, blocks)
+    activations, input_grad_t, weight_grad = pl.pallas_call(
+        keep_kernel,
+        out_shape=tuple(jax.ShapeDtypeStruct(x.shape, x.dtype) for x in outs),
+        in_specs=[vmem()] * 3,
+        out_specs=(vmem(),) * 3,
+    )(*outs)
+    return activations, input_grad_t.T, weight_grad
 
 
 def fits(mesh, features, weight, cotangent, block_values):
@@ -425,7 +438,8 @@
     rows, cols = cotangent.shape[0] // nrow, features.shape[0] // group
     tile = rows * cols * 2 + block_values.shape[2] * 128 * 128 * 6
     moved = 8 * rows * width + 12 * cols * width
-    whole = nrep % 2 == 0 and 128 % fw == 0 and (width // nrow) % (8 * group) == 0
+    whole = nrep % 2 == 0 and block_values.shape[2] == 128 and rows * cols % 128**3 == 0
+    whole = whole and (width // nrow) % (8 * group) == 0
     return whole and nrow > 1 and group > 2 and tile + moved < VMEM_BUDGET * 3 // 4
 
 

time: 68.6 us -> 61.2 us (0.89)
  local copies, waits for them, and re-layouts: 6.71 us -> 0 us
  other arithmetic: 2.23 us -> 0 us
  Pallas kernels: 58 us -> 59.7 us
    unnamed x3 -> x0, local copies, waits for them, and re-layouts: 4.98 us -> none
    pallas_call x0 -> x1, Pallas kernels: none -> 1.88 us  [local_kernel(): pl.pallas_call(keep_kernel, out_shape=tuple((jax.ShapeDtypeStruct(x.shape...]
    pallas_call x1 -> x0, local copies, waits for them, and re-layouts: 1.73 us -> none  [local_kernel(): pl.pallas_call(functools.partial(layer_kernel, sizes), out_shape=(jax.Sha...]
    reduce_max x1 -> x0, other arithmetic: 0.78 us -> none  [local_kernel(): table = jnp.max(jnp.where(hit, slot[None, :] + 1, 0), axis=1)]
    add x2 -> x0, other arithmetic: 0.76 us -> none  [the longest x1 0.76 us: local_kernel(): place = coords[:, 0] * col_blocks + coords[:, 1]]
where the time goes in v2:
time: 61.2 us; the launch traced here: 61 us
  Pallas kernels  59.7 us (98%)
  between operations  1.29 us (2%)
    pallas_call x1, Pallas kernels, local_kernel(): pl.pallas_call(functools.partial(layer_kernel, sizes), out_shape=(jax.Sha...  57.9 us
    pallas_call x1, Pallas kernels, local_kernel(): pl.pallas_call(keep_kernel, out_shape=tuple((jax.ShapeDtypeStruct(x.shape...  1.88 us

profile of v2, /device:TPU:0, one launch (start us, length us, event | category | flops | bytes accessed | tf_op | source)
XLA Modules:
  0.0 61.0 jit_solution(4261926325364963574)
XLA Ops:
  1.3 57.9 %shard_map.85 = (bf16[256,256]{1,0:T(8,128)(2,1)}, bf16[64,1024]{1,0:T(8,128)(2,1)}, f32[256,256]{1,0:T(8,128)}) custom-call(s32[1,1]{1,0:T(1,128)S(6)} %copy.9.count_in, s32[2,128]{1,0:T(2,128)} %bitcast.8, bf16[64,1024]{1,0:T(8,128)(2,1)} %bitcast.7, bf16[256,256]{1,0:T(8,128)(2,1)} %weight_in.1, bf16[256,256]{1,0:T(8,128)(2,1)} %cot_in.1, ...), custom_call_target="tpu_custom_call" | custom-call | tf_op jit(solution)/shard_map/pallas_call | solution.py:367
  59.1 1.9 %shard_map.86 = (bf16[256,256]{1,0:T(8,128)(2,1)}, bf16[64,1024]{1,0:T(8,128)(2,1)}, f32[256,256]{1,0:T(8,128)}) custom-call(bf16[256,256]{1,0:T(8,128)(2,1)} %get-tuple-element.9.a_in, bf16[64,1024]{1,0:T(8,128)(2,1)} %get-tuple-element.10.b_in, f32[256,256]{1,0:T(8,128)} %get-tuple-element.11.c_in), custom_call_target="tpu_custom_call" | custom-call | tf_op jit(solution)/shard_map/pallas_call | solution.py:424

commit v3 on v2

--- a/solution.py
+++ b/solution.py
@@ -114,7 +114,6 @@
     shard_buf,
     srec,
     wall,
-    wgather,
     tvec,
     table,
     load_sem,
@@ -128,7 +127,6 @@
     w_sem,
     s_sem,
     g_sem,
-    h_sem,
 ):
     nrow, ncol, nrep = sizes
     nh = nrep // 2
@@ -163,6 +161,16 @@
         dc, dh = offsets[i]
         return ((c + ncol - dc) % ncol) * nrep + ((h + nh - dh) % nh) * 2 + core
 
+    def nearest(n):
+        code = 0
+        for q in range(nrow):
+            order = sorted(range(nrow), key=lambda t: (abs(t - q), t))
+            code += order[n] * nrow**q
+        power = 1
+        for q in range(1, nrow):
+            power = power * jnp.where(r >= q, nrow, 1)
+        return (code // power) % nrow
+
     def rcopy(src, dst, sems, i, device):
         return pltpu.make_async_remote_copy(
             src_ref=src,
@@ -189,9 +197,14 @@
 
     pl.semaphore_wait(barrier, nrow - 1 + group - 1)
     fcopies = []
-    for j in range(1, nrow):
-        fcopies.append(rcopy(feat_in, fbuf.at[r], f_sem, j - 1, to_row(j)))
-        fcopies[-1].start()
+    for side in range(2):
+        there = r > 0 if side == 0 else r < nrow - 1
+        copy = rcopy(feat_in, fbuf.at[r], f_sem.at[side], r, {"row": (r + nrow - 1 + 2 * side) % nrow})
+        fcopies.append((there, copy))
+
+        @pl.when(there)
+        def _(copy=copy):
+            copy.start()
 
     fbuf[r] = feat_in[...]
 
@@ -230,33 +243,65 @@
 
     lax.fori_loop(0, row_blocks, fill, 0)
 
-    for copy in fcopies:
-        copy.wait()
-    feat[...] = fbuf[...].reshape(width, col_nodes).T
-
-    def partial(part):
-        return dot(dense[pl.ds(part * nodes, nodes), :], feat[...])
-
-    pcopies = []
-    for i in range(chips):
-        pbuf[i] = partial(part_to(i, 1 - k)).astype(BF16)
-        pcopies.append(rcopy(pbuf.at[i], prec.at[i], p_sem, i, {"rep": partner}))
-        pcopies[i].start()
+    half = nodes // 2
+
+    def partial(part, slot):
+        x = dot(dense[pl.ds(part * nodes, nodes), :], fbuf[slot], 1, 1)
+        return jnp.concatenate([x[:half], x[half:]], axis=1)
+
     qcopies = []
-    for i in range(chips - 1):
-        mine = partial(part_to(i, k))
-        pcopies[i].wait()
-        qbuf[i] = (mine + prec[i].astype(F32)).astype(BF16)
-        qcopies.append(rcopy(qbuf.at[i], qrec.at[i], q_sem, i, to_chip(i)))
-        qcopies[i].start()
-    summed = partial(g)
-    pcopies[chips - 1].wait()
-    summed = summed + prec[chips - 1].astype(F32)
-    for i in reversed(range(chips - 1)):
-        qcopies[i].wait()
-        summed = summed + qrec[i].astype(F32)
-
-    aggregate = summed.astype(BF16)
+
+    def merge(n, pcopy, mine):
+        pcopy.wait()
+        for i in range(chips - 1):
+            qbuf[n, i] = (mine[i] + prec[n, i].astype(F32)).astype(BF16)
+            copy = rcopy(qbuf.at[n, i], qrec.at[n, i], q_sem.at[n], i, to_chip(i))
+            copy.start()
+            qcopies.append(copy)
+        return mine[chips - 1] + prec[n, chips - 1].astype(F32)
+
+    held, waiting = [], None
+    for n in range(nrow):
+        slot = nearest(n)
+        if n > 0:
+            side = (slot < r).astype(jnp.int32)
+            there = jnp.where(slot < r, r < nrow - 1, r > 0)
+            copy = rcopy(
+                fbuf.at[slot], fbuf.at[slot], f_sem.at[side], slot, {"row": (r + nrow - 1 + 2 * side) % nrow}
+            )
+            copy.wait_recv()
+            fcopies.append((there, copy))
+
+            @pl.when(there)
+            def _(copy=copy):
+                copy.start()
+
+        for i in range(chips):
+            pbuf[n, i] = partial(part_to(i, 1 - k), slot).astype(BF16)
+        pcopy = rcopy(pbuf.at[n], prec.at[n], p_sem, n, {"rep": partner})
+        pcopy.start()
+        if waiting is not None:
+            held.append(merge(*waiting))
+        waiting = (n, pcopy, [partial(part_to(i, k), slot) for i in range(chips)])
+    held.append(merge(*waiting))
+    for there, copy in fcopies:
+
+        @pl.when(there)
+        def _(copy=copy):
+            copy.wait_send()
+
+    for n in range(nrow):
+        got = held[n]
+        for i in range(chips - 1):
+            qcopies[n * (chips - 1) + i].wait()
+            got = got + qrec[n, i].astype(F32)
+        feat[nearest(n)] = got.astype(BF16)
+
+    spread = jnp.concatenate([feat[m] for m in range(nrow)], axis=1)
+    pieces = [spread[:, m * fw : (m + 1) * fw] for m in range(2 * nrow)]
+    aggregate = jnp.concatenate(
+        [jnp.concatenate(pieces[0::2], axis=1), jnp.concatenate(pieces[1::2], axis=1)], axis=0
+    )
     pre_act = dot(aggregate, weight_in[...])
     sigma = jax.nn.sigmoid(pre_act)
     grad_pre = (cot_in[...].astype(F32) * sigma * (1.0 + pre_act * (1.0 - sigma))).astype(BF16)
@@ -269,11 +314,11 @@
     first.start()
 
     terms = dot(aggregate, grad_pre, 0, 0)
-    wrows = width // nrow
-    wbuf[...] = terms.astype(BF16).reshape(nrow, wrows, width)
+    srows = width // group
+    wbuf[...] = terms.astype(BF16).reshape(group, srows, width)
     wcopies = []
-    for j in range(1, nrow):
-        wcopies.append(rcopy(wbuf.at[(r + j) % nrow], wrec.at[j - 1], w_sem, j - 1, to_row(j)))
+    for j in range(1, group):
+        wcopies.append(rcopy(wbuf.at[(g + j) % group], wrec.at[j - 1], w_sem, j - 1, to_group(j)))
         wcopies[-1].start()
     act_out[...] = (pre_act * sigma).astype(BF16)
 
@@ -283,18 +328,6 @@
     total[...] = back_term(own_back[...], g)
     first.wait()
     total[...] += back_term(bpar[chips - 1], c * nrep + partner)
-
-    for copy in wcopies:
-        copy.wait()
-    share = wbuf[r].astype(F32)
-    for j in range(nrow - 1):
-        share = share + wrec[j].astype(F32)
-    srows = wrows // group
-    shard_buf[...] = share.reshape(group, srows, width)
-    scopies = []
-    for j in range(1, group):
-        scopies.append(rcopy(shard_buf.at[(g + j) % group], srec.at[j - 1], s_sem, j - 1, to_group(j)))
-        scopies[-1].start()
 
     for i in reversed(range(chips - 1)):
         bcopies[i].wait()
@@ -302,16 +335,15 @@
         ccopies[-1].start()
         total[...] += back_term(brec[i], part_from(i, k))
 
-    for copy in scopies:
-        copy.wait()
-    final = shard_buf[g]
+    share = wbuf[g].astype(F32)
     for j in range(group - 1):
-        final = final + srec[j]
-    wall[g] = final
-    gcopies = []
-    for j in range(1, group):
-        gcopies.append(rcopy(wall.at[g], wall.at[g], g_sem, j - 1, to_group(j)))
-        gcopies[-1].start()
+        wcopies[j].wait()
+        share = share + wrec[j].astype(F32)
+    shard_buf[...] = share.astype(BF16)
+    scopies = []
+    for j in range(1, nrow):
+        scopies.append(rcopy(shard_buf, srec.at[j - 1], s_sem, j - 1, to_row(j)))
+        scopies[-1].start()
 
     for n, i in enumerate(reversed(range(chips - 1))):
         ccopies[n].wait()
@@ -324,22 +356,23 @@
         zcopies.append(rcopy(zbuf.at[j - 1], zrec.at[j - 1], z_sem, j - 1, to_row(j)))
         zcopies[-1].start()
 
-    for copy in gcopies:
-        copy.wait()
-    wgather[r] = wall[...].reshape(wrows, width)
-    hcopies = []
-    for j in range(1, nrow):
-        hcopies.append(rcopy(wgather.at[r], wgather.at[r], h_sem, j - 1, to_row(j)))
-        hcopies[-1].start()
+    for j in range(nrow - 1):
+        scopies[j].wait()
+        share = share + srec[j].astype(F32)
+    wall[g] = share
+    gcopies = []
+    for j in range(1, group):
+        gcopies.append(rcopy(wall.at[g], wall.at[g], g_sem, j - 1, to_group(j)))
+        gcopies[-1].start()
 
     mine = total[pl.ds(r * fw, fw), :]
     for j in range(nrow - 1):
         zcopies[j].wait()
         mine = mine + zrec[j].astype(F32)
     igrad_out[...] = mine.astype(BF16)
-    for copy in hcopies:
+    for copy in gcopies:
         copy.wait()
-    wgrad_out[...] = wgather[...].reshape(width, width)
+    wgrad_out[...] = wall[...].reshape(width, width)
 
 
 def keep_kernel(a_in, b_in, c_in, a_out, b_out, c_out):
@@ -359,9 +392,9 @@
     row_blocks = nodes * group // 128
     places = row_blocks * (col_nodes // 128)
     chunks = math.gcd(slots, 8)
-    wrows = width // nrow
-    srows = wrows // group
+    srows = width // group
     square = (nodes, width)
+    half = (nodes // 2, 2 * fw)
     vmem = functools.partial(pl.BlockSpec, memory_space=pltpu.VMEM)
     dma = pltpu.SemaphoreType.DMA
     outs = pl.pallas_call(
@@ -385,37 +418,35 @@
             pltpu.VMEM((slots, 128, 128), BF16),
             pltpu.VMEM((slots + 1, 128, 128), F32),
             pltpu.VMEM((row_blocks * 128, col_nodes), BF16),
-            pltpu.VMEM((col_nodes, width), BF16),
-            pltpu.VMEM((chips,) + square, BF16),
-            pltpu.VMEM((chips,) + square, BF16),
-            pltpu.VMEM((chips - 1,) + square, BF16),
-            pltpu.VMEM((chips - 1,) + square, BF16),
+            pltpu.VMEM((nrow,) + half, BF16),
+            pltpu.VMEM((nrow, chips) + half, BF16),
+            pltpu.VMEM((nrow, chips) + half, BF16),
+            pltpu.VMEM((nrow, chips - 1) + half, BF16),
+            pltpu.VMEM((nrow, chips - 1) + half, BF16),
             pltpu.VMEM((width, nodes), BF16),
             pltpu.VMEM((chips - 1, width, nodes), BF16),
             pltpu.VMEM((chips, width, nodes), BF16),
             pltpu.VMEM((width, col_nodes), F32),
             pltpu.VMEM((nrow - 1, fw, col_nodes), BF16),
             pltpu.VMEM((nrow - 1, fw, col_nodes), BF16),
-            pltpu.VMEM((nrow, wrows, width), BF16),
-            pltpu.VMEM((nrow - 1, wrows, width), BF16),
+            pltpu.VMEM((group, srows, width), BF16),
+            pltpu.VMEM((group - 1, srows, width), BF16),
+            pltpu.VMEM((srows, width), BF16),
+            pltpu.VMEM((nrow - 1, srows, width), BF16),
             pltpu.VMEM((group, srows, width), F32),
-            pltpu.VMEM((group - 1, srows, width), F32),
-            pltpu.VMEM((group, srows, width), F32),
-            pltpu.VMEM((nrow, wrows, width), F32),
             pltpu.VMEM((1, slots + places), jnp.int32),
             pltpu.SMEM((1, slots + places), jnp.int32),
             dma((chunks,)),
             dma,
-            dma((2, nrow - 1)),
-            dma((2, chips)),
-            dma((2, chips - 1)),
+            dma((2, 2, nrow)),
+            dma((2, nrow)),
+            dma((nrow, 2, chips - 1)),
             dma((2, chips - 1)),
             dma((2, chips)),
             dma((2, nrow - 1)),
+            dma((2, group - 1)),
             dma((2, nrow - 1)),
             dma((2, group - 1)),
-            dma((2, group - 1)),
-            dma((2, nrow - 1)),
         ],
         compiler_params=pltpu.CompilerParams(
             collective_id=0, has_side_effects=True, vmem_limit_bytes=VMEM_BUDGET
@@ -439,7 +470,7 @@
     tile = rows * cols * 2 + block_values.shape[2] * 128 * 128 * 6
     moved = 8 * rows * width + 12 * cols * width
     whole = nrep % 2 == 0 and block_values.shape[2] == 128 and rows * cols % 128**3 == 0
-    whole = whole and (width // nrow) % (8 * group) == 0
+    whole = whole and 2 * fw == 128 and width % (16 * group) == 0
     return whole and nrow > 1 and group > 2 and tile + moved < VMEM_BUDGET * 3 // 4
 
 

time: 61.2 us -> 51.3 us (0.84)
  Pallas kernels: 59.7 us -> 49.9 us
    pallas_call x1, Pallas kernels: 57.9 us -> 48 us  [local_kernel(): pl.pallas_call(functools.partial(layer_kernel, sizes), out_shape=(jax.Sha...]
where the time goes in v3:
time: 51.3 us; the launch traced here: 51.2 us
  Pallas kernels  49.9 us (97%)
  between operations  1.29 us (3%)
    pallas_call x1, Pallas kernels, local_kernel(): pl.pallas_call(functools.partial(layer_kernel, sizes), out_shape=(jax.Sha...  48 us
    pallas_call x1, Pallas kernels, local_kernel(): pl.pallas_call(keep_kernel, out_shape=tuple((jax.ShapeDtypeStruct(x.shape...  1.88 us

profile of v3, /device:TPU:0, one launch (start us, length us, event | category | flops | bytes accessed | tf_op | source)
XLA Modules:
  0.0 51.2 jit_solution(16584680417059395806)
XLA Ops:
  1.3 48.0 %shard_map.85 = (bf16[256,256]{1,0:T(8,128)(2,1)}, bf16[64,1024]{1,0:T(8,128)(2,1)}, f32[256,256]{1,0:T(8,128)}) custom-call(s32[1,1]{1,0:T(1,128)S(6)} %copy.9.count_in, s32[2,128]{1,0:T(2,128)} %bitcast.8, bf16[64,1024]{1,0:T(8,128)(2,1)} %bitcast.7, bf16[256,256]{1,0:T(8,128)(2,1)} %weight_in.1, bf16[256,256]{1,0:T(8,128)(2,1)} %cot_in.1, ...), custom_call_target="tpu_custom_call" | custom-call | tf_op jit(solution)/shard_map/pallas_call | solution.py:400
  49.3 1.9 %shard_map.86 = (bf16[256,256]{1,0:T(8,128)(2,1)}, bf16[64,1024]{1,0:T(8,128)(2,1)}, f32[256,256]{1,0:T(8,128)}) custom-call(bf16[256,256]{1,0:T(8,128)(2,1)} %get-tuple-element.9.a_in, bf16[64,1024]{1,0:T(8,128)(2,1)} %get-tuple-element.10.b_in, f32[256,256]{1,0:T(8,128)} %get-tuple-element.11.c_in), custom_call_target="tpu_custom_call" | custom-call | tf_op jit(solution)/shard_map/pallas_call | solution.py:455

commit v4 on v3

--- a/solution.py
+++ b/solution.py
@@ -305,13 +305,18 @@
     pre_act = dot(aggregate, weight_in[...])
     sigma = jax.nn.sigmoid(pre_act)
     grad_pre = (cot_in[...].astype(F32) * sigma * (1.0 + pre_act * (1.0 - sigma))).astype(BF16)
-    own_back[...] = dot(weight_in[...], grad_pre, 1, 1).astype(BF16)
-    bcopies, ccopies = [], []
-    for i in range(chips - 1):
-        bcopies.append(rcopy(own_back, brec.at[i], b_sem, i, to_chip(i)))
-        bcopies[i].start()
-    first = rcopy(own_back, bpar.at[chips - 1], c_sem, chips - 1, {"rep": partner})
-    first.start()
+    own_back[...] = dot(weight_in[...], grad_pre, 1, 1).astype(BF16).reshape(nrow, fw, nodes)
+    bcopies, ccopies, firsts = [], [], []
+    for m in range(nrow):
+        q = nearest(nrow - 1 - m)
+        bcopies.append([])
+        for i in range(chips - 1):
+            bcopies[m].append(rcopy(own_back.at[q], brec.at[m, i], b_sem.at[m], i, to_chip(i)))
+            bcopies[m][i].start()
+        firsts.append(
+            rcopy(own_back.at[q], bpar.at[m, chips - 1], c_sem.at[m], chips - 1, {"rep": partner})
+        )
+        firsts[m].start()
 
     terms = dot(aggregate, grad_pre, 0, 0)
     srows = width // group
@@ -325,36 +330,70 @@
     def back_term(piece_t, part):
         return dot(piece_t, dense[pl.ds(part * nodes, nodes), :])
 
-    total[...] = back_term(own_back[...], g)
-    first.wait()
-    total[...] += back_term(bpar[chips - 1], c * nrep + partner)
-
-    for i in reversed(range(chips - 1)):
-        bcopies[i].wait()
-        ccopies.append(rcopy(brec.at[i], bpar.at[i], c_sem, i, {"rep": partner}))
-        ccopies[-1].start()
-        total[...] += back_term(brec[i], part_from(i, k))
-
-    share = wbuf[g].astype(F32)
-    for j in range(group - 1):
-        wcopies[j].wait()
-        share = share + wrec[j].astype(F32)
-    shard_buf[...] = share.astype(BF16)
-    scopies = []
-    for j in range(1, nrow):
-        scopies.append(rcopy(shard_buf, srec.at[j - 1], s_sem, j - 1, to_row(j)))
-        scopies[-1].start()
-
-    for n, i in enumerate(reversed(range(chips - 1))):
-        ccopies[n].wait()
-        total[...] += back_term(bpar[i], part_from(i, 1 - k))
-
+    def pass_on(m):
+        ccopies.append([])
+        for i in reversed(range(chips - 1)):
+            bcopies[m][i].wait()
+            copy = rcopy(brec.at[m, i], bpar.at[m, i], c_sem.at[m], i, {"rep": partner})
+            copy.start()
+            ccopies[m].append(copy)
+
+    def compute(m):
+        own = back_term(own_back[nearest(nrow - 1 - m)], g)
+        for i in reversed(range(chips - 1)):
+            own = own + back_term(brec[m, i], part_from(i, k))
+        firsts[m].wait()
+        own = own + back_term(bpar[m, chips - 1], c * nrep + partner)
+        for n, i in enumerate(reversed(range(chips - 1))):
+            ccopies[m][n].wait()
+            own = own + back_term(bpar[m, i], part_from(i, 1 - k))
+        total[m] = own
+
+    zparts = zbuf.shape[1]
+    zcols = col_nodes // zparts
     zcopies = []
-    for j in range(1, nrow):
-        q = (r + j) % nrow
-        zbuf[j - 1] = total[pl.ds(q * fw, fw), :].astype(BF16)
-        zcopies.append(rcopy(zbuf.at[j - 1], zrec.at[j - 1], z_sem, j - 1, to_row(j)))
-        zcopies[-1].start()
+
+    def chain(m, later):
+        q = nearest(nrow - 1 - m)
+        side = (q > r).astype(jnp.int32)
+        joined = jnp.where(q > r, r > 0, r < nrow - 1)
+        target = {"row": (r + nrow - 1 + 2 * side) % nrow}
+
+        @pl.when(joined if later else jnp.logical_not(joined))
+        def _():
+            for e in range(zparts):
+                copy = rcopy(zbuf.at[q, e], zrec.at[side, q, e], z_sem.at[side, e], q, target)
+                mine = total[m, :, e * zcols : (e + 1) * zcols]
+                if later:
+                    copy.wait_recv()
+                    mine = mine + zrec[side, q, e].astype(F32)
+                zbuf[q, e] = mine.astype(BF16)
+                copy.start()
+
+        if later:
+            for e in range(zparts):
+                zcopies.append(rcopy(zbuf.at[q, e], zrec.at[side, q, e], z_sem.at[side, e], q, target))
+
+    for m in range(nrow):
+        if m < 2:
+            pass_on(m)
+        if 1 <= m < nrow - 1:
+            pass_on(m + 1)
+        compute(m)
+        if m < nrow - 1:
+            chain(m, False)
+        if m > 0:
+            chain(m - 1, True)
+        if m == 1:
+            share = wbuf[g].astype(F32)
+            for j in range(group - 1):
+                wcopies[j].wait()
+                share = share + wrec[j].astype(F32)
+            shard_buf[...] = share.astype(BF16)
+            scopies = []
+            for j in range(1, nrow):
+                scopies.append(rcopy(shard_buf, srec.at[j - 1], s_sem, j - 1, to_row(j)))
+                scopies[-1].start()
 
     for j in range(nrow - 1):
         scopies[j].wait()
@@ -365,11 +404,21 @@
         gcopies.append(rcopy(wall.at[g], wall.at[g], g_sem, j - 1, to_group(j)))
         gcopies[-1].start()
 
-    mine = total[pl.ds(r * fw, fw), :]
-    for j in range(nrow - 1):
-        zcopies[j].wait()
-        mine = mine + zrec[j].astype(F32)
-    igrad_out[...] = mine.astype(BF16)
+    for side in range(2):
+
+        @pl.when(r > 0 if side == 1 else r < nrow - 1)
+        def _(side=side):
+            for e in range(zparts):
+                came = rcopy(
+                    zbuf.at[r, e], zrec.at[side, r, e], z_sem.at[side, e], r, {"row": (r + 1) % nrow}
+                )
+                came.wait_recv()
+                cols = slice(e * zcols, (e + 1) * zcols)
+                total[nrow - 1, :, cols] = total[nrow - 1, :, cols] + zrec[side, r, e].astype(F32)
+
+    igrad_out[...] = total[nrow - 1].astype(BF16)
+    for copy in zcopies:
+        copy.wait_send()
     for copy in gcopies:
         copy.wait()
     wgrad_out[...] = wall[...].reshape(width, width)
@@ -394,6 +443,7 @@
     chunks = math.gcd(slots, 8)
     srows = width // group
     square = (nodes, width)
+    zparts = 2
     half = (nodes // 2, 2 * fw)
     vmem = functools.partial(pl.BlockSpec, memory_space=pltpu.VMEM)
     dma = pltpu.SemaphoreType.DMA
@@ -423,12 +473,12 @@
             pltpu.VMEM((nrow, chips) + half, BF16),
             pltpu.VMEM((nrow, chips - 1) + half, BF16),
             pltpu.VMEM((nrow, chips - 1) + half, BF16),
-            pltpu.VMEM((width, nodes), BF16),
-            pltpu.VMEM((chips - 1, width, nodes), BF16),
-            pltpu.VMEM((chips, width, nodes), BF16),
-            pltpu.VMEM((width, col_nodes), F32),
-            pltpu.VMEM((nrow - 1, fw, col_nodes), BF16),
-            pltpu.VMEM((nrow - 1, fw, col_nodes), BF16),
+            pltpu.VMEM((nrow, fw, nodes), BF16),
+            pltpu.VMEM((nrow, chips - 1, fw, nodes), BF16),
+            pltpu.VMEM((nrow, chips, fw, nodes), BF16),
+            pltpu.VMEM((nrow, fw, col_nodes), F32),
+            pltpu.VMEM((nrow, zparts, fw, col_nodes // zparts), BF16),
+            pltpu.VMEM((2, nrow, zparts, fw, col_nodes // zparts), BF16),
             pltpu.VMEM((group, srows, width), BF16),
             pltpu.VMEM((group - 1, srows, width), BF16),
             pltpu.VMEM((srows, width), BF16),
@@ -441,9 +491,9 @@
             dma((2, 2, nrow)),
             dma((2, nrow)),
             dma((nrow, 2, chips - 1)),
-            dma((2, chips - 1)),
-            dma((2, chips)),
-            dma((2, nrow - 1)),
+            dma((nrow, 2, chips - 1)),
+            dma((nrow, 2, chips)),
+            dma((2, zparts, 2, nrow)),
             dma((2, group - 1)),
             dma((2, nrow - 1)),
             dma((2, group - 1)),

time: 51.3 us -> 52.6 us (1.025)
  Pallas kernels: 49.9 us -> 51.1 us
    pallas_call x1, Pallas kernels: 48 us -> 49.3 us  [local_kernel(): pl.pallas_call(functools.partial(layer_kernel, sizes), out_shape=(jax.Sha...]
where the time goes in v4:
time: 52.6 us; the launch traced here: 52.4 us
  Pallas kernels  51.1 us (97%)
  between operations  1.29 us (2%)
    pallas_call x1, Pallas kernels, local_kernel(): pl.pallas_call(functools.partial(layer_kernel, sizes), out_shape=(jax.Sha...  49.3 us
    pallas_call x1, Pallas kernels, local_kernel(): pl.pallas_call(keep_kernel, out_shape=tuple((jax.ShapeDtypeStruct(x.shape...  1.88 us

profile of v4, /device:TPU:0, one launch (start us, length us, event | category | flops | bytes accessed | tf_op | source)
XLA Modules:
  0.0 52.4 jit_solution(12668388884943694289)
XLA Ops:
  1.3 49.3 %shard_map.85 = (bf16[256,256]{1,0:T(8,128)(2,1)}, bf16[64,1024]{1,0:T(8,128)(2,1)}, f32[256,256]{1,0:T(8,128)}) custom-call(s32[1,1]{1,0:T(1,128)S(6)} %copy.9.count_in, s32[2,128]{1,0:T(2,128)} %bitcast.8, bf16[64,1024]{1,0:T(8,128)(2,1)} %bitcast.7, bf16[256,256]{1,0:T(8,128)(2,1)} %weight_in.1, bf16[256,256]{1,0:T(8,128)(2,1)} %cot_in.1, ...), custom_call_target="tpu_custom_call" | custom-call | tf_op jit(solution)/shard_map/pallas_call | solution.py:450
  50.5 1.9 %shard_map.86 = (bf16[256,256]{1,0:T(8,128)(2,1)}, bf16[64,1024]{1,0:T(8,128)(2,1)}, f32[256,256]{1,0:T(8,128)}) custom-call(bf16[256,256]{1,0:T(8,128)(2,1)} %get-tuple-element.9.a_in, bf16[64,1024]{1,0:T(8,128)(2,1)} %get-tuple-element.10.b_in, f32[256,256]{1,0:T(8,128)} %get-tuple-element.11.c_in), custom_call_target="tpu_custom_call" | custom-call | tf_op jit(solution)/shard_map/pallas_call | solution.py:505

commit v5 on v4

--- a/solution.py
+++ b/solution.py
@@ -317,14 +317,15 @@
             rcopy(own_back.at[q], bpar.at[m, chips - 1], c_sem.at[m], chips - 1, {"rep": partner})
         )
         firsts[m].start()
-
-    terms = dot(aggregate, grad_pre, 0, 0)
-    srows = width // group
-    wbuf[...] = terms.astype(BF16).reshape(group, srows, width)
-    wcopies = []
-    for j in range(1, group):
-        wcopies.append(rcopy(wbuf.at[(g + j) % group], wrec.at[j - 1], w_sem, j - 1, to_group(j)))
-        wcopies[-1].start()
+        if m == 0:
+            terms = dot(aggregate, grad_pre, 0, 0)
+            srows = width // group
+            wbuf[...] = terms.astype(BF16).reshape(group, srows, width)
+            wcopies = []
+            for j in range(1, group):
+                wcopies.append(rcopy(wbuf.at[(g + j) % group], wrec.at[j - 1], w_sem, j - 1, to_group(j)))
+                wcopies[-1].start()
+
     act_out[...] = (pre_act * sigma).astype(BF16)
 
     def back_term(piece_t, part):
@@ -382,9 +383,7 @@
         compute(m)
         if m < nrow - 1:
             chain(m, False)
-        if m > 0:
-            chain(m - 1, True)
-        if m == 1:
+        if m == 0:
             share = wbuf[g].astype(F32)
             for j in range(group - 1):
                 wcopies[j].wait()
@@ -394,15 +393,17 @@
             for j in range(1, nrow):
                 scopies.append(rcopy(shard_buf, srec.at[j - 1], s_sem, j - 1, to_row(j)))
                 scopies[-1].start()
-
-    for j in range(nrow - 1):
-        scopies[j].wait()
-        share = share + srec[j].astype(F32)
-    wall[g] = share
-    gcopies = []
-    for j in range(1, group):
-        gcopies.append(rcopy(wall.at[g], wall.at[g], g_sem, j - 1, to_group(j)))
-        gcopies[-1].start()
+        else:
+            chain(m - 1, True)
+        if m == 2:
+            for j in range(nrow - 1):
+                scopies[j].wait()
+                share = share + srec[j].astype(F32)
+            wall[g] = share
+            gcopies = []
+            for j in range(1, group):
+                gcopies.append(rcopy(wall.at[g], wall.at[g], g_sem, j - 1, to_group(j)))
+                gcopies[-1].start()
 
     for side in range(2):
 
@@ -520,7 +521,7 @@
     tile = rows * cols * 2 + block_values.shape[2] * 128 * 128 * 6
     moved = 8 * rows * width + 12 * cols * width
     whole = nrep % 2 == 0 and block_values.shape[2] == 128 and rows * cols % 128**3 == 0
-    whole = whole and 2 * fw == 128 and width % (16 * group) == 0
+    whole = whole and 2 * fw == 128 and nrow > 2 and width % (16 * group) == 0
     return whole and nrow > 1 and group > 2 and tile + moved < VMEM_BUDGET * 3 // 4
 
 

time: 52.6 us -> 53.7 us (1.021)
  Pallas kernels: 51.1 us -> 52.2 us
    pallas_call x1, Pallas kernels: 49.3 us -> 50.4 us  [local_kernel(): pl.pallas_call(functools.partial(layer_kernel, sizes), out_shape=(jax.Sha...]
where the time goes in v5:
time: 53.7 us; the launch traced here: 53.5 us
  Pallas kernels  52.2 us (97%)
  between operations  1.29 us (2%)
    pallas_call x1, Pallas kernels, local_kernel(): pl.pallas_call(functools.partial(layer_kernel, sizes), out_shape=(jax.Sha...  50.4 us
    pallas_call x1, Pallas kernels, local_kernel(): pl.pallas_call(keep_kernel, out_shape=tuple((jax.ShapeDtypeStruct(x.shape...  1.88 us

profile of v5, /device:TPU:0, one launch (start us, length us, event | category | flops | bytes accessed | tf_op | source)
XLA Modules:
  0.0 53.5 jit_solution(3023116240450696169)
XLA Ops:
  1.3 50.4 %shard_map.85 = (bf16[256,256]{1,0:T(8,128)(2,1)}, bf16[64,1024]{1,0:T(8,128)(2,1)}, f32[256,256]{1,0:T(8,128)}) custom-call(s32[1,1]{1,0:T(1,128)S(6)} %copy.9.count_in, s32[2,128]{1,0:T(2,128)} %bitcast.8, bf16[64,1024]{1,0:T(8,128)(2,1)} %bitcast.7, bf16[256,256]{1,0:T(8,128)(2,1)} %weight_in.1, bf16[256,256]{1,0:T(8,128)(2,1)} %cot_in.1, ...), custom_call_target="tpu_custom_call" | custom-call | tf_op jit(solution)/shard_map/pallas_call | solution.py:451
  51.7 1.9 %shard_map.86 = (bf16[256,256]{1,0:T(8,128)(2,1)}, bf16[64,1024]{1,0:T(8,128)(2,1)}, f32[256,256]{1,0:T(8,128)}) custom-call(bf16[256,256]{1,0:T(8,128)(2,1)} %get-tuple-element.9.a_in, bf16[64,1024]{1,0:T(8,128)(2,1)} %get-tuple-element.10.b_in, f32[256,256]{1,0:T(8,128)} %get-tuple-element.11.c_in), custom_call_target="tpu_custom_call" | custom-call | tf_op jit(solution)/shard_map/pallas_call | solution.py:506

commit v6 on v3

--- a/solution.py
+++ b/solution.py
@@ -206,6 +206,20 @@
         def _(copy=copy):
             copy.start()
 
+    def relay(n):
+        slot = nearest(n)
+        side = (slot < r).astype(jnp.int32)
+        there = jnp.where(slot < r, r < nrow - 1, r > 0)
+        copy = rcopy(
+            fbuf.at[slot], fbuf.at[slot], f_sem.at[side], slot, {"row": (r + nrow - 1 + 2 * side) % nrow}
+        )
+        copy.wait_recv()
+        fcopies.append((there, copy))
+
+        @pl.when(there)
+        def _():
+            copy.start()
+
     fbuf[r] = feat_in[...]
 
     places = row_blocks * col_blocks
@@ -234,6 +248,9 @@
             return carry
 
         lax.fori_loop(i * per, (i + 1) * per, add_slot, 0)
+        if i == chunks // 2 - 1:
+            relay(1)
+    relay(2)
 
     def fill(rb, carry):
         for cb in range(col_blocks):
@@ -263,19 +280,6 @@
     held, waiting = [], None
     for n in range(nrow):
         slot = nearest(n)
-        if n > 0:
-            side = (slot < r).astype(jnp.int32)
-            there = jnp.where(slot < r, r < nrow - 1, r > 0)
-            copy = rcopy(
-                fbuf.at[slot], fbuf.at[slot], f_sem.at[side], slot, {"row": (r + nrow - 1 + 2 * side) % nrow}
-            )
-            copy.wait_recv()
-            fcopies.append((there, copy))
-
-            @pl.when(there)
-            def _(copy=copy):
-                copy.start()
-
         for i in range(chips):
             pbuf[n, i] = partial(part_to(i, 1 - k), slot).astype(BF16)
         pcopy = rcopy(pbuf.at[n], prec.at[n], p_sem, n, {"rep": partner})
@@ -283,6 +287,8 @@
         if waiting is not None:
             held.append(merge(*waiting))
         waiting = (n, pcopy, [partial(part_to(i, k), slot) for i in range(chips)])
+        if 3 <= n + 2 < nrow:
+            relay(n + 2)
     held.append(merge(*waiting))
     for there, copy in fcopies:
 
@@ -470,7 +476,7 @@
     tile = rows * cols * 2 + block_values.shape[2] * 128 * 128 * 6
     moved = 8 * rows * width + 12 * cols * width
     whole = nrep % 2 == 0 and block_values.shape[2] == 128 and rows * cols % 128**3 == 0
-    whole = whole and 2 * fw == 128 and width % (16 * group) == 0
+    whole = whole and 2 * fw == 128 and nrow > 2 and width % (16 * group) == 0
     return whole and nrow > 1 and group > 2 and tile + moved < VMEM_BUDGET * 3 // 4
 
 

time: 51.3 us -> 52 us (1.014)
  Pallas kernels: 49.9 us -> 50.5 us
    pallas_call x1, Pallas kernels: 48 us -> 48.6 us  [local_kernel(): pl.pallas_call(functools.partial(layer_kernel, sizes), out_shape=(jax.Sha...]
where the time goes in v6:
time: 52 us; the launch traced here: 51.8 us
  Pallas kernels  50.5 us (97%)
  between operations  1.29 us (2%)
    pallas_call x1, Pallas kernels, local_kernel(): pl.pallas_call(functools.partial(layer_kernel, sizes), out_shape=(jax.Sha...  48.6 us
    pallas_call x1, Pallas kernels, local_kernel(): pl.pallas_call(keep_kernel, out_shape=tuple((jax.ShapeDtypeStruct(x.shape...  1.88 us

profile of v6, /device:TPU:0, one launch (start us, length us, event | category | flops | bytes accessed | tf_op | source)
XLA Modules:
  0.0 51.8 jit_solution(15915456963974223862)
XLA Ops:
  1.3 48.6 %shard_map.85 = (bf16[256,256]{1,0:T(8,128)(2,1)}, bf16[64,1024]{1,0:T(8,128)(2,1)}, f32[256,256]{1,0:T(8,128)}) custom-call(s32[1,1]{1,0:T(1,128)S(6)} %copy.9.count_in, s32[2,128]{1,0:T(2,128)} %bitcast.8, bf16[64,1024]{1,0:T(8,128)(2,1)} %bitcast.7, bf16[256,256]{1,0:T(8,128)(2,1)} %weight_in.1, bf16[256,256]{1,0:T(8,128)(2,1)} %cot_in.1, ...), custom_call_target="tpu_custom_call" | custom-call | tf_op jit(solution)/shard_map/pallas_call | solution.py:406
  49.9 1.9 %shard_map.86 = (bf16[256,256]{1,0:T(8,128)(2,1)}, bf16[64,1024]{1,0:T(8,128)(2,1)}, f32[256,256]{1,0:T(8,128)}) custom-call(bf16[256,256]{1,0:T(8,128)(2,1)} %get-tuple-element.9.a_in, bf16[64,1024]{1,0:T(8,128)(2,1)} %get-tuple-element.10.b_in, f32[256,256]{1,0:T(8,128)} %get-tuple-element.11.c_in), custom_call_target="tpu_custom_call" | custom-call | tf_op jit(solution)/shard_map/pallas_call | solution.py:461
